TPU v7x, 32 devices: a whole 2x2x4 slice. The times are simulated.
32 devices in a mesh: grp: 4 (over x, core), ep: 4 (over z), sq: 2 (over y).
Axes of the slice: x: 2, y: 2, z: 4, core: 2. Of those that a mesh axis runs over, the one named last changes fastest.
Arguments:
- queries: bfloat16 [8192, 2048], P(('grp', 'ep', 'sq')), may hold values from -32 to 32
- keys: bfloat16 [8192, 512], P(('grp', 'ep', 'sq')), may hold values from -32 to 32
- values: bfloat16 [8192, 512], P(('grp', 'ep', 'sq')), may hold values from -6 to 6
- norm_gain: float32 [2048], replicated, may hold values from 0.1 to 1.9
- expert_ids: int32 [8192, 2], P(('grp', 'ep', 'sq')), may hold values from 0 to 3, all different within a row; in each aligned block of 256 rows (0 to 255, 256 to 511, ...) at most 192 rows name the same one
- gate_values: float32 [8192, 2], P(('grp', 'ep', 'sq')), may hold values from 0.1 to 1
- hidden_grad: bfloat16 [8192, 1024], P(('grp', 'ep', 'sq')), may hold values from -0.59765625 to 0.59765625
- gate_weight: bfloat16 [4, 2048, 1024], P('ep', None, 'sq'), may hold values from -0.125 to 0.125
- up_weight: bfloat16 [4, 2048, 1024], P('ep', None, 'sq'), may hold values from -0.125 to 0.125
Outputs:
- gate_grad: float32 [4, 2048, 1024], P('ep', 'grp', 'sq')
Inputs may be any that keep to these rules, and one draw needn't show every extreme that they name: `expert_ids`: each token names 2 different experts; within the 256 tokens of one device no expert is named more than 192 times.
All inputs are finite; a program needn't handle non-finite values.
Results may differ from a plain program's by a relative error of at most 0.0085.
Values may be sent and summed in bfloat16 or wider, within the bound.
A program may use at most 64 MiB of HBM per device.

v0:
```python
import math
import jax
import jax.numpy as jnp
from jax import lax
from jax.sharding import PartitionSpec as P

HEAD_DIM = 128
LENGTH = 512
epsilon = 1e-05
masked_score = -1e30


def gate_term(inputs, cotangent, weight_gate, weight_up):
    pre_gate = jnp.dot(inputs, weight_gate, preferred_element_type=jnp.float32)
    pre_up = jnp.dot(inputs, weight_up, preferred_element_type=jnp.float32)
    sigmoid_gate = jax.nn.sigmoid(pre_gate)
    slope = sigmoid_gate * (1.0 + pre_gate * (1.0 - sigmoid_gate))
    delta_gate = (cotangent.astype(jnp.float32) * pre_up * slope).astype(jnp.bfloat16)
    return lax.dot_general(
        inputs, delta_gate, (((0,), (0,)), ((), ())), preferred_element_type=jnp.float32
    )


def body(
    queries, keys, values, norm_gain, expert_ids, gate_values, hidden_grad, gate_weight, up_weight
):
    rows_here, model_width = queries.shape
    kv_width = keys.shape[1]
    kv_heads = kv_width // HEAD_DIM
    group_size = model_width // kv_width
    score_scale = 1.0 / math.sqrt(HEAD_DIM)
    shard_index = lax.axis_index("sq")
    query_positions = shard_index * rows_here + jnp.arange(rows_here, dtype=jnp.int32)
    query_sequence = query_positions // LENGTH
    query_heads = queries.reshape(rows_here, kv_heads, group_size, HEAD_DIM)
    running_max = jnp.full((rows_here, kv_heads, group_size), masked_score, jnp.float32)
    key_rows = lax.all_gather(keys, "sq", axis=0, tiled=True)
    value_rows = lax.all_gather(values, "sq", axis=0, tiled=True)
    key_count = key_rows.shape[0]
    key_heads = key_rows.reshape(key_count, kv_heads, HEAD_DIM)
    value_heads = value_rows.reshape(key_count, kv_heads, HEAD_DIM)
    scores = (
        jnp.einsum("tkgd,rkd->tkgr", query_heads, key_heads, preferred_element_type=jnp.float32)
        * score_scale
    )
    key_positions = jnp.arange(key_count, dtype=jnp.int32)
    causal = key_positions[None, :] <= query_positions[:, None]
    same_sequence = (key_positions // LENGTH)[None, :] == query_sequence[:, None]
    allowed = (causal & same_sequence)[:, None, None, :]
    scores = jnp.where(allowed, scores, masked_score)
    updated_max = jnp.maximum(running_max, jnp.max(scores, axis=-1))
    exponent_terms = jnp.where(allowed, jnp.exp(scores - updated_max[..., None]), 0.0)
    running_sum = jnp.sum(exponent_terms, axis=-1)
    running_out = jnp.einsum(
        "tkgr,rkd->tkgd",
        exponent_terms.astype(jnp.bfloat16),
        value_heads,
        preferred_element_type=jnp.float32,
    )
    attended = (running_out / running_sum[..., None]).reshape(rows_here, model_width)
    mean_square = jnp.mean(attended * attended, axis=-1, keepdims=True)
    normed = (attended * lax.rsqrt(mean_square + epsilon) * norm_gain).astype(jnp.bfloat16)
    top_count = expert_ids.shape[1]
    experts = lax.axis_size("ep")
    capacity = rows_here * top_count // experts * 3 // 2
    hidden_width = hidden_grad.shape[1]
    flat_ids = expert_ids.reshape(-1)
    one_hot = (flat_ids[:, None] == jnp.arange(experts, dtype=jnp.int32)[None, :]).astype(jnp.int32)
    slot_rank = jnp.sum(jnp.cumsum(one_hot, axis=0) * one_hot, axis=1) - 1
    slot_target = flat_ids * capacity + slot_rank
    routed_inputs = jnp.repeat(normed, top_count, axis=0)
    routed_grad = (
        gate_values.reshape(-1, 1) * jnp.repeat(hidden_grad, top_count, axis=0).astype(jnp.float32)
    ).astype(jnp.bfloat16)
    send_inputs = (
        jnp.zeros((experts * capacity, model_width), jnp.bfloat16)
        .at[slot_target]
        .set(routed_inputs)
    )
    send_grad = (
        jnp.zeros((experts * capacity, hidden_width), jnp.bfloat16).at[slot_target].set(routed_grad)
    )
    send_inputs = send_inputs.reshape(experts, capacity, model_width)
    send_grad = send_grad.reshape(experts, capacity, hidden_width)
    got_inputs, got_grad = (
        lax.all_to_all(send_inputs, "ep", split_axis=0, concat_axis=0, tiled=True),
        lax.all_to_all(send_grad, "ep", split_axis=0, concat_axis=0, tiled=True),
    )
    expert_inputs = got_inputs.reshape(-1, model_width)
    expert_grad = got_grad.reshape(-1, hidden_width)
    weight_gate = gate_weight[0]
    weight_up = up_weight[0]
    local_hidden = weight_gate.shape[1]
    column_start = shard_index * local_hidden
    input_rows = lax.all_gather(expert_inputs, "sq", axis=0, tiled=True)
    grad_rows = lax.all_gather(expert_grad, "sq", axis=0, tiled=True)
    cotangent = lax.dynamic_slice_in_dim(grad_rows, column_start, local_hidden, 1)
    summed = gate_term(input_rows, cotangent, weight_gate, weight_up)
    return lax.psum_scatter(
        summed[None].astype(jnp.bfloat16), "grp", scatter_dimension=1, tiled=True
    ).astype(jnp.float32)


def solution(mesh):
    return jax.shard_map(
        body,
        mesh=mesh,
        in_specs=(
            P(("grp", "ep", "sq"), None),
            P(("grp", "ep", "sq"), None),
            P(("grp", "ep", "sq"), None),
            P(),
            P(("grp", "ep", "sq"), None),
            P(("grp", "ep", "sq"), None),
            P(("grp", "ep", "sq"), None),
            P("ep", None, "sq"),
            P("ep", None, "sq"),
        ),
        out_specs=P("ep", "grp", "sq"),
        check_vma=False,
    )
```

profile of v0, /device:TPU:0, one launch (start us, length us, event | category | flops | bytes accessed | tf_op | source)
XLA Modules:
  0.0 312.1 jit_solution(6690040816627483020)
XLA Ops:
  8.8 1.2 reduce-window.6
  10.5 1.1 copy.17
  11.6 10.0 %all_gather.12 = bf16[512,512]{0,1:T(8,128)(2,1)} all-gather(bf16[256,512]{0,1:T(8,128)(2,1)S(1)} %copy.17), channel_id=1, replica_groups=mesh['grp'=4,'ep'=4,'sq'=2] {'sq'}, dimensions={0}, use_global_device_ids=true | all-gather | bytes 786432 | tf_op jit(solution)/shard_map/all_gather | solution.py:37
  21.7 8.4 %all_gather.13 = bf16[512,512]{1,0:T(8,128)(2,1)S(1)} all-gather(bf16[256,512]{1,0:T(8,128)(2,1)} %param.11), channel_id=1, replica_groups=mesh['grp'=4,'ep'=4,'sq'=2] {'sq'}, dimensions={0}, use_global_device_ids=true | all-gather | bytes 786432 | tf_op jit(solution)/shard_map/all_gather | solution.py:38
  31.0 1.8 reshape.173
  33.0 2.7 fusion
  35.8 2.0 fusion.1
  37.8 2.5 multiply_reduce_fusion
  40.3 1.3 fusion.13
  41.7 1.5 copy.22
  43.1 2.6 broadcast_in_dim.51
  45.8 4.1 %reshape.185 = bf16[512,2048]{1,0:T(8,128)(2,1)} reshape(bf16[256,2,2048]{2,1,0:T(2,128)(2,1)} %broadcast_in_dim.51) | data formatting | bytes 4194304 | tf_op jit(solution)/shard_map/reshape | solution.py:71
  49.9 6.7 %scatter_custom_fusion = bf16[768,2048]{1,0:T(8,128)(2,1)} fusion(s32[512]{0:T(512)S(1)} %bitcast.79, bf16[512,2048]{1,0:T(8,128)(2,1)} %reshape.185, bf16[]{:T(256)} %constant.25.clone.1), kind=kCustom, calls=%fused_computation.23 | custom fusion | bytes 3146240 | tf_op jit(solution)/shard_map/scatter | solution.py:78
  56.6 74.8 %all_to_all.10 = bf16[4,192,2048]{2,1,0:T(8,128)(2,1)} all-to-all(bf16[4,192,2048]{2,1,0:T(8,128)(2,1)} %bitcast.72), channel_id=1, replica_groups=mesh['grp'=4,'ep'=4,'sq'=2] {'ep'}, dimensions={0} | all-to-all | bytes 6291456 | tf_op jit(solution)/shard_map/all_to_all | solution.py:86
  132.5 2.0 broadcast_in_dim.53
  134.4 3.7 %convert_element_type.40 = f32[512,1024]{1,0:T(8,128)} reshape(f32[256,2,1024]{2,1,0:T(2,128)} %broadcast_in_dim.53) | data formatting | bytes 4194304 | tf_op jit(solution)/shard_map/convert_element_type | solution.py:73
  138.1 5.3 %scatter_custom_fusion.1 = bf16[768,1024]{1,0:T(8,128)(2,1)} fusion(s32[512]{0:T(512)S(1)} %bitcast.80, f32[512,1024]{1,0:T(8,128)} %convert_element_type.40, f32[512]{0:T(512)S(1)} %mul.89, bf16[]{:T(256)} %constant.25.clone.1), kind=kCustom, calls=%fused_computation.25 | custom fusion | flops 1048576 | bytes 3672066 | tf_op jit(solution)/shard_map/scatter | solution.py:81
  143.4 40.3 %all_to_all.11 = bf16[4,192,1024]{2,1,0:T(8,128)(2,1)} all-to-all(bf16[4,192,1024]{2,1,0:T(8,128)(2,1)} %bitcast.74), channel_id=1, replica_groups=mesh['grp'=4,'ep'=4,'sq'=2] {'ep'}, dimensions={0} | all-to-all | bytes 3145728 | tf_op jit(solution)/shard_map/all_to_all | solution.py:87
  183.7 26.9 %all-gather.3.cloned.1.call-done = bf16[1536,2048]{1,0:T(8,128)(2,1)} async-done(((bf16[768,2048]{1,0:T(8,128)(2,1)}), bf16[1536,2048]{1,0:T(8,128)(2,1)}) %all-gather.3.cloned.1.call-update) | async-done | bytes 6291472 | tf_op jit(solution)/shard_map/all_gather | solution.py:95
  210.7 8.5 %fusion.9 = f32[1536,512]{1,0:T(8,128)} fusion(bf16[1536,2048]{1,0:T(8,128)(2,1)} %all-gather.3.cloned.1.call-done, bf16[1,2048,512]{2,1,0:T(8,128)(2,1)} %param.16), kind=kOutput, calls=%fused_computation.14 | convolution fusion | flops 3221225472 | bytes 11534336 | tf_op jit(solution)/shard_map/dot_general | solution.py:14
  219.2 38.0 %all-gather.5.cloned.1.call-done = bf16[1536,1024]{1,0:T(8,128)(2,1)} async-done(((bf16[768,1024]{1,0:T(8,128)(2,1)}), bf16[1536,1024]{1,0:T(8,128)(2,1)}) %all-gather.5.cloned.1.call-update) | async-done | bytes 3145744 | tf_op jit(solution)/shard_map/all_gather | solution.py:96
  257.2 14.6 %fusion.8 = bf16[1,2048,512]{2,1,0:T(8,128)(2,1)} fusion(bf16[1536,2048]{1,0:T(8,128)(2,1)} %all-gather.3.cloned.1.call-done, f32[1536,512]{1,0:T(8,128)} %fusion.9, bf16[1,2048,512]{2,1,0:T(8,128)(2,1)S(1)} %copy-done, bf16[1536,1024]{1,0:T(8,128)(2,1)} %all-gather.5.cloned.1.call-done, s32[]{:T(128)S(6)} %select_n.44), kind=kOutput, calls=%fused_computation.13 | convolution fusion | flops 6452150272 | bytes 21495812 | tf_op jit(solution)/shard_map/dot_general | solution.py:19
  271.8 31.6 %reduce-scatter.2.cloned.1.call-done = bf16[1,512,512]{2,1,0:T(8,128)(2,1)} async-done(((bf16[1,2048,512]{2,1,0:T(8,128)(2,1)}), bf16[1,512,512]{2,1,0:T(8,128)(2,1)}) %reduce-scatter.2.cloned.1.call-update) | async-done | bytes 524304 | tf_op jit(solution)/shard_map/reduce_scatter | solution.py:99
  303.4 2.1 convert_element_type.46
  (37 shorter events, 5.0 us)
Async XLA Ops:
  6.5 250.7 %copy-start = (bf16[1,2048,512]{2,1,0:T(8,128)(2,1)S(1)}, bf16[1,2048,512]{2,1,0:T(8,128)(2,1)}, u32[]{:S(2)}) copy-start(bf16[1,2048,512]{2,1,0:T(8,128)(2,1)} %param.17) | copy-start | bytes 6291460
  6.5 204.1 %all-gather.3.cloned.1.call-start = ((), (), s32[]{:S(2)}) async-start(), calls=%async_computation.3 | async-start | bytes 9437184 | tf_op jit(solution)/shard_map/all_gather | solution.py:95
  35.8 2.0 copy-start.2
  37.8 2.5 copy-start.3
  131.4 0.7 copy-start.4
  131.4 1.1 copy-start.1
  131.4 125.8 %all-gather.5.cloned.1.call-start = ((), (), s32[]{:S(2)}) async-start(), calls=%async_computation.4 | async-start | bytes 4718592 | tf_op jit(solution)/shard_map/all_gather | solution.py:96
  183.7 119.7 %reduce-scatter.2.cloned.1.call-start = ((), (), s32[]{:S(2)}) async-start(), calls=%async_computation.5 | async-start | bytes 2621440 | tf_op jit(solution)/shard_map/reduce_scatter | solution.py:99
Sparse Core Ops, SparseCore 0:
  131.6 79.0 all-gather.2
  212.2 44.9 all-gather.4
  272.0 31.4 reduce-scatter.1
where the time goes:
time: 313 us; the launch traced here: 312 us
  blocking collectives  133 us (42%)
  waiting for transfers between devices  96.5 us (31%)
  matrix products  28.4 us (9%)
  local copies, waits for them, and re-layouts  27 us (9%)
  other arithmetic  13.3 us (4%)
  between operations  13.3 us (4%)
    all_to_all x1, blocking collectives, body(): lax.all_to_all(send_inputs, 'ep', split_axis=0, concat_axis=0, tiled=True)  74.8 us
    all_to_all x1, blocking collectives, body(): lax.all_to_all(send_grad, 'ep', split_axis=0, concat_axis=0, tiled=True)  40.3 us
    all_gather x1, waiting for transfers between devices, body(): grad_rows = lax.all_gather(expert_grad, 'sq', axis=0, tiled=True)  38 us
    reduce_scatter x1, waiting for transfers between devices, body(): lax.psum_scatter(summed[None].astype(jnp.bfloat16), 'grp', scatter_dimens...  31.6 us
    all_gather x1, waiting for transfers between devices, body(): input_rows = lax.all_gather(expert_inputs, 'sq', axis=0, tiled=True)  26.9 us
    dot_general x1, matrix products, gate_term(): lax.dot_general(inputs, delta_gate, (((0,), (0,)), ((), ())), preferred_e...  14.6 us
    all_gather x1, blocking collectives, body(): key_rows = lax.all_gather(keys, 'sq', axis=0, tiled=True)  10 us
    dot_general x1, matrix products, gate_term(): pre_gate = jnp.dot(inputs, weight_gate, preferred_element_type=jnp.float32)  8.55 us
  transfers between devices with their start and end apart: 3, of which 3 were waited for; matrix products, arithmetic and copies ran while one was open for 6% of the time, Pallas kernels for 0%

commit v1 on v0

--- a/solution.py
+++ b/solution.py
@@ -1,3 +1,4 @@
+import functools
 import math
 import jax
 import jax.numpy as jnp
@@ -8,6 +9,27 @@
 LENGTH = 512
 epsilon = 1e-05
 masked_score = -1e30
+
+
+def _form_lines(raw, dim_at, ndim_at):
+    local_out, top = (jax.lax.axis_size("ep"), jax.lax.axis_index("ep"))
+    block_next = raw.shape[dim_at] // local_out
+    heard = list(raw.shape)
+    heard[dim_at] = block_next
+    w_next = heard[ndim_at]
+    heard[ndim_at] = w_next * local_out
+    p = 0
+    shaped = jnp.zeros(heard, raw.dtype)
+    while p < local_out:
+        p_next = lax.dynamic_slice_in_dim(raw, (top ^ p) * block_next, block_next, axis=dim_at)
+        if p:
+            p_next = jax.lax.ppermute(p_next, "ep", perm=[(u, u ^ p) for u in range(local_out)])
+        shaped = lax.dynamic_update_slice_in_dim(shaped, p_next, (top ^ p) * w_next, axis=ndim_at)
+        p += 1
+    return shaped
+
+
+refer_table = functools.partial(_form_lines, dim_at=0, ndim_at=0)
 
 
 def gate_term(inputs, cotangent, weight_gate, weight_up):
@@ -83,7 +105,7 @@
     send_inputs = send_inputs.reshape(experts, capacity, model_width)
     send_grad = send_grad.reshape(experts, capacity, hidden_width)
     got_inputs, got_grad = (
-        lax.all_to_all(send_inputs, "ep", split_axis=0, concat_axis=0, tiled=True),
+        refer_table(send_inputs),
         lax.all_to_all(send_grad, "ep", split_axis=0, concat_axis=0, tiled=True),
     )
     expert_inputs = got_inputs.reshape(-1, model_width)

time: 313 us -> 319 us (1.019)
  blocking collectives: 133 us -> 68.5 us
  waiting for transfers between devices: 96.5 us -> 152 us
  local copies, waits for them, and re-layouts: 27 us -> 34.1 us
  starting transfers between devices: 0.09 us -> 4.47 us
    all_to_all x1 -> x0, blocking collectives: 74.8 us -> none  [body(): lax.all_to_all(send_inputs, 'ep', split_axis=0, concat_axis=0, tiled=True)]
    ppermute x0 -> x3, waiting for transfers between devices: none -> 51.2 us  [_form_lines(): jax.lax.ppermute(p_next, 'ep', perm=[(u, u ^ p) for u in range(local_out)])]
    all_to_all x1, blocking collectives: 40.3 us -> 50.4 us  [body(): lax.all_to_all(send_grad, 'ep', split_axis=0, concat_axis=0, tiled=True)]
    ppermute x0 -> x3, starting transfers between devices: none -> 4.39 us  [_form_lines(): jax.lax.ppermute(p_next, 'ep', perm=[(u, u ^ p) for u in range(local_out)])]
    all_gather x1, waiting for transfers between devices: 26.9 us -> 31.1 us  [body(): input_rows = lax.all_gather(expert_inputs, 'sq', axis=0, tiled=True)]
  transfers between devices with their start and end apart: 3 -> 6, of which waited for: 3 -> 5; matrix products, arithmetic and copies ran while one was open for 6% -> 7% of each run, Pallas kernels for 0% -> 0%
where the time goes in v1:
time: 319 us; the launch traced here: 318 us
  waiting for transfers between devices  152 us (48%)
  blocking collectives  68.5 us (21%)
  local copies, waits for them, and re-layouts  34.1 us (11%)
  matrix products  30.5 us (10%)
  other arithmetic  15.4 us (5%)
  between operations  13.3 us (4%)
  starting transfers between devices  4.47 us (1%)
    ppermute x3, waiting for transfers between devices, _form_lines(): jax.lax.ppermute(p_next, 'ep', perm=[(u, u ^ p) for u in range(local_out)])  51.2 us
    all_to_all x1, blocking collectives, body(): lax.all_to_all(send_grad, 'ep', split_axis=0, concat_axis=0, tiled=True)  50.4 us
    all_gather x1, waiting for transfers between devices, body(): grad_rows = lax.all_gather(expert_grad, 'sq', axis=0, tiled=True)  38 us
    reduce_scatter x1, waiting for transfers between devices, body(): lax.psum_scatter(summed[None].astype(jnp.bfloat16), 'grp', scatter_dimens...  31.6 us
    all_gather x1, waiting for transfers between devices, body(): input_rows = lax.all_gather(expert_inputs, 'sq', axis=0, tiled=True)  31.1 us
    dot_general x1, matrix products, gate_term(): lax.dot_general(inputs, delta_gate, (((0,), (0,)), ((), ())), preferred_e...  14.6 us
    all_gather x1, blocking collectives, body(): key_rows = lax.all_gather(keys, 'sq', axis=0, tiled=True)  9.94 us
    dot_general x1, matrix products, gate_term(): pre_gate = jnp.dot(inputs, weight_gate, preferred_element_type=jnp.float32)  8.48 us
  transfers between devices with their start and end apart: 6, of which 5 were waited for; matrix products, arithmetic and copies ran while one was open for 7% of the time, Pallas kernels for 0%

profile of v1, /device:TPU:0, one launch (start us, length us, event | category | flops | bytes accessed | tf_op | source)
XLA Modules:
  0.0 318.2 jit_solution(6170619024243081111)
XLA Ops:
  8.5 1.8 reshape.173
  11.4 9.9 %all_gather.12 = bf16[512,512]{0,1:T(8,128)(2,1)S(1)} all-gather(bf16[256,512]{0,1:T(8,128)(2,1)S(1)} %copy.17), channel_id=1, replica_groups=mesh['grp'=4,'ep'=4,'sq'=2] {'sq'}, dimensions={0}, use_global_device_ids=true | all-gather | bytes 786432 | tf_op jit(solution)/shard_map/all_gather | solution.py:59
  21.5 4.9 %fusion = (f32[256,4,4]{0,2,1:T(4,128)S(1)}, f32[4,512,256,4]{2,1,3,0:T(8,128)}) fusion(pred[256,512]{0,1:T(8,128)(4,1)S(1)} %fusion.25, bf16[512,4,128,1]{0,2,3,1:T(8,128)(2,1)S(1)} %bitcast.72, bf16[256,4,4,128]{3,2,1,0:T(4,128)(2,1)S(1)} %reshape.173), kind=kOutput, calls=%fused_computation.4 | convolution fusion | flops 543158272 | bytes 10108928 | tf_op jit(solution)/shard_map/tkgd,rkd->tkgr/dot_general | solution.py:65
  26.4 8.2 %all_gather.13 = bf16[512,512]{1,0:T(8,128)(2,1)S(1)} all-gather(bf16[256,512]{1,0:T(8,128)(2,1)S(1)} %copy-done.4), channel_id=1, replica_groups=mesh['grp'=4,'ep'=4,'sq'=2] {'sq'}, dimensions={0}, use_global_device_ids=true | all-gather | bytes 786432 | tf_op jit(solution)/shard_map/all_gather | solution.py:60
  34.8 4.6 %fusion.1 = f32[256,4,4]{0,2,1:T(4,128)S(1)} fusion(f32[4,512,256,4]{2,1,3,0:T(8,128)} %get-tuple-element.10, f32[256,4,4]{0,2,1:T(4,128)S(1)} %broadcast_maximum_fusion, pred[256,512]{0,1:T(8,128)(4,1)S(1)} %fusion.25), kind=kLoop, calls=%fused_computation.5 | loop fusion | flops 10481664 | bytes 8552448 | tf_op jit(solution)/shard_map/reduce_sum | solution.py:75
  40.7 2.5 multiply_reduce_fusion
  46.0 2.6 broadcast_in_dim.55
  48.6 4.1 %reshape.185 = bf16[512,2048]{1,0:T(8,128)(2,1)} reshape(bf16[256,2,2048]{2,1,0:T(2,128)(2,1)} %broadcast_in_dim.55) | data formatting | bytes 4194304 | tf_op jit(solution)/shard_map/reshape | solution.py:93
  54.8 6.7 %scatter_custom_fusion = bf16[768,2048]{1,0:T(8,128)(2,1)} fusion(s32[512]{0:T(512)S(1)} %bitcast.76, bf16[512,2048]{1,0:T(8,128)(2,1)} %reshape.185, bf16[]{:T(256)} %constant.25.clone.1), kind=kCustom, calls=%fused_computation.23 | custom fusion | bytes 3146240 | tf_op jit(solution)/shard_map/scatter | solution.py:100
  61.5 2.0 broadcast_in_dim.49
  65.8 1.5 collective-permute-start
  67.3 2.6 collective-permute-start.1
  70.1 28.6 %collective-permute-done = bf16[1,192,2048]{2,1,0:T(8,128)(2,1)S(1)} collective-permute-done((bf16[1,192,2048]{2,1,0:T(8,128)(2,1)S(1)}, bf16[1,192,2048]{2,1,0:T(8,128)(2,1)S(1)}, u32[]{:S(2)}, u32[]{:S(2)}) %collective-permute-start) | collective-permute-done | bytes 786464 | tf_op jit(solution)/shard_map/ppermute | solution.py:26
  99.7 22.6 %collective-permute-done.1 = bf16[1,192,2048]{2,1,0:T(8,128)(2,1)S(1)} collective-permute-done((bf16[1,192,2048]{2,1,0:T(8,128)(2,1)S(1)}, bf16[1,192,2048]{2,1,0:T(8,128)(2,1)S(1)}, u32[]{:S(2)}, u32[]{:S(2)}) %collective-permute-start.1) | collective-permute-done | bytes 786464 | tf_op jit(solution)/shard_map/ppermute | solution.py:26
  124.4 1.9 broadcast_in_dim.57
  126.3 3.7 %convert_element_type.40 = f32[512,1024]{1,0:T(8,128)} reshape(f32[256,2,1024]{2,1,0:T(2,128)} %broadcast_in_dim.57) | data formatting | bytes 4194304 | tf_op jit(solution)/shard_map/convert_element_type | solution.py:95
  130.3 4.9 %scatter_custom_fusion.1 = bf16[768,1024]{1,0:T(8,128)(2,1)} fusion(s32[512]{0:T(512)S(1)} %bitcast.77, f32[512,1024]{1,0:T(8,128)} %convert_element_type.40, f32[512]{0:T(512)S(1)} %mul.89, bf16[]{:T(256)} %constant.25.clone.1), kind=kCustom, calls=%fused_computation.25 | custom fusion | flops 1048576 | bytes 3672066 | tf_op jit(solution)/shard_map/scatter | solution.py:103
  135.2 50.4 %all_to_all.5 = bf16[4,192,1024]{2,1,0:T(8,128)(2,1)} all-to-all(bf16[4,192,1024]{2,1,0:T(8,128)(2,1)} %bitcast.71), channel_id=1, replica_groups=mesh['grp'=4,'ep'=4,'sq'=2] {'ep'}, dimensions={0} | all-to-all | bytes 3145728 | tf_op jit(solution)/shard_map/all_to_all | solution.py:109
  185.7 31.1 %all-gather.3.cloned.1.call-done = bf16[1536,2048]{1,0:T(8,128)(2,1)} async-done(((bf16[768,2048]{1,0:T(8,128)(2,1)}), bf16[1536,2048]{1,0:T(8,128)(2,1)}) %all-gather.3.cloned.1.call-update) | async-done | bytes 6291472 | tf_op jit(solution)/shard_map/all_gather | solution.py:117
  216.8 8.5 %fusion.9 = f32[1536,512]{1,0:T(8,128)} fusion(bf16[1536,2048]{1,0:T(8,128)(2,1)} %all-gather.3.cloned.1.call-done, bf16[1,2048,512]{2,1,0:T(8,128)(2,1)} %param.16), kind=kOutput, calls=%fused_computation.14 | convolution fusion | flops 3221225472 | bytes 11534336 | tf_op jit(solution)/shard_map/dot_general | solution.py:36
  225.2 38.0 %all-gather.5.cloned.1.call-done = bf16[1536,1024]{1,0:T(8,128)(2,1)} async-done(((bf16[768,1024]{1,0:T(8,128)(2,1)}), bf16[1536,1024]{1,0:T(8,128)(2,1)}) %all-gather.5.cloned.1.call-update) | async-done | bytes 3145744 | tf_op jit(solution)/shard_map/all_gather | solution.py:118
  263.3 14.6 %fusion.8 = bf16[1,2048,512]{2,1,0:T(8,128)(2,1)} fusion(bf16[1536,2048]{1,0:T(8,128)(2,1)} %all-gather.3.cloned.1.call-done, f32[1536,512]{1,0:T(8,128)} %fusion.9, bf16[1,2048,512]{2,1,0:T(8,128)(2,1)S(1)} %copy-done, bf16[1536,1024]{1,0:T(8,128)(2,1)} %all-gather.5.cloned.1.call-done, s32[]{:T(128)S(6)} %select_n.64), kind=kOutput, calls=%fused_computation.13 | convolution fusion | flops 6452150272 | bytes 21495812 | tf_op jit(solution)/shard_map/dot_general | solution.py:41
  277.9 31.6 %reduce-scatter.2.cloned.1.call-done = bf16[1,512,512]{2,1,0:T(8,128)(2,1)} async-done(((bf16[1,2048,512]{2,1,0:T(8,128)(2,1)}), bf16[1,512,512]{2,1,0:T(8,128)(2,1)}) %reduce-scatter.2.cloned.1.call-update) | async-done | bytes 524304 | tf_op jit(solution)/shard_map/reduce_scatter | solution.py:121
  309.5 2.1 convert_element_type.46
  (51 shorter events, 15.4 us)
Async XLA Ops:
  6.5 256.7 %copy-start = (bf16[1,2048,512]{2,1,0:T(8,128)(2,1)S(1)}, bf16[1,2048,512]{2,1,0:T(8,128)(2,1)}, u32[]{:S(2)}) copy-start(bf16[1,2048,512]{2,1,0:T(8,128)(2,1)} %param.17) | copy-start | bytes 6291460
  6.5 210.2 %all-gather.3.cloned.1.call-start = ((), (), s32[]{:S(2)}) async-start(), calls=%async_computation.2 | async-start | bytes 9437184 | tf_op jit(solution)/shard_map/all_gather | solution.py:117
  21.5 4.9 %copy-start.4 = (bf16[256,512]{1,0:T(8,128)(2,1)S(1)}, bf16[256,512]{1,0:T(8,128)(2,1)}, u32[]{:S(2)}) copy-start(bf16[256,512]{1,0:T(8,128)(2,1)} %param.11) | copy-start | bytes 786436
  34.8 5.8 %copy-start.1 = (f32[4,512,256,4]{2,1,3,0:T(8,128)S(1)}, f32[4,512,256,4]{2,1,3,0:T(8,128)}, u32[]{:S(2)}) copy-start(f32[4,512,256,4]{2,1,3,0:T(8,128)} %get-tuple-element.10) | copy-start | bytes 25165828
  40.7 2.5 copy-start.5
  61.5 3.0 copy-start.2
  65.8 33.0 %collective-permute-start = (bf16[1,192,2048]{2,1,0:T(8,128)(2,1)S(1)}, bf16[1,192,2048]{2,1,0:T(8,128)(2,1)S(1)}, u32[]{:S(2)}, u32[]{:S(2)}) collective-permute-start(bf16[1,192,2048]{2,1,0:T(8,128)(2,1)S(1)} %get-tuple-element.7), channel_id=1, source_target_pairs={{0,2},{2,0},{4,6},{6,4},{1,3},{3,1},{5,7},{7,5},{8,10},{10,8},{12,... | collective-permute-start | bytes 2359304 | tf_op jit(solution)/shard_map/ppermute | solution.py:26
  67.3 55.1 %collective-permute-start.1 = (bf16[1,192,2048]{2,1,0:T(8,128)(2,1)S(1)}, bf16[1,192,2048]{2,1,0:T(8,128)(2,1)S(1)}, u32[]{:S(2)}, u32[]{:S(2)}) collective-permute-start(bf16[1,192,2048]{2,1,0:T(8,128)(2,1)S(1)} %get-tuple-element.6), channel_id=1, source_target_pairs={{0,4},{2,6},{4,0},{6,2},{1,5},{3,7},{5,1},{7,3},{8,12},{10,14},{12... | collective-permute-start | bytes 2359304 | tf_op jit(solution)/shard_map/ppermute | solution.py:26
  69.8 53.5 %collective-permute-start.2 = (bf16[1,192,2048]{2,1,0:T(8,128)(2,1)S(1)}, bf16[1,192,2048]{2,1,0:T(8,128)(2,1)S(1)}, u32[]{:S(2)}, u32[]{:S(2)}) collective-permute-start(bf16[1,192,2048]{2,1,0:T(8,128)(2,1)S(1)} %get-tuple-element.5), channel_id=1, source_target_pairs={{0,6},{2,4},{4,2},{6,0},{1,7},{3,5},{5,3},{7,1},{8,14},{10,12},{12... | collective-permute-start | bytes 2359304 | tf_op jit(solution)/shard_map/ppermute | solution.py:26
  99.7 24.7 %copy-start.3 = (bf16[256,1024]{1,0:T(8,128)(2,1)S(1)}, bf16[256,1024]{1,0:T(8,128)(2,1)}, u32[]{:S(2)}) copy-start(bf16[256,1024]{1,0:T(8,128)(2,1)} %param.15) | copy-start | bytes 1572868
  124.3 5.6 %copy-start.6 = (f32[256,2]{0,1:T(2,128)S(1)}, f32[256,2]{0,1:T(2,128)}, u32[]{:S(2)}) copy-start(f32[256,2]{0,1:T(2,128)} %param.14) | copy-start | bytes 6148
  124.4 138.9 %all-gather.5.cloned.1.call-start = ((), (), s32[]{:S(2)}) async-start(), calls=%async_computation.3 | async-start | bytes 4718592 | tf_op jit(solution)/shard_map/all_gather | solution.py:118
  185.6 123.9 %reduce-scatter.2.cloned.1.call-start = ((), (), s32[]{:S(2)}) async-start(), calls=%async_computation.4 | async-start | bytes 2621440 | tf_op jit(solution)/shard_map/reduce_scatter | solution.py:121
Sparse Core Ops, SparseCore 0:
  124.5 92.2 all-gather.2
  218.3 44.9 all-gather.4
  278.0 31.4 reduce-scatter.1
